TPU v7x, 128 devices: a whole 4x4x4 slice. The times are simulated.
128 devices in a mesh: enc: 8 (over z, core), gen: 16 (over x, y).
Axes of the slice: x: 4, y: 4, z: 4, core: 2. Of those that a mesh axis runs over, the one named last changes fastest.
Arguments:
- hidden_states: bfloat16 [8192, 4096], P('gen'), may hold values from -60 to 60
- grad_out: bfloat16 [8192, 4096], P('gen'), may hold values from -0.29882812 to 0.29882812
- nbr_embed: bfloat16 [256, 128, 1024], P(('enc', 'gen')), may hold values from -60 to 60
- nbr_index: int32 [128, 2], replicated, may hold values from 0 to 255, as said below
- gain: float32 [4096], replicated, may hold values from 0.5 to 1.5
- w_query: bfloat16 [4096, 4096], P(None, 'enc'), may hold values from -0.1875 to 0.1875
- w_out: bfloat16 [4096, 4096], P('enc'), may hold values from -0.09375 to 0.09375
- w_key: bfloat16 [1024, 4096], P(None, 'enc'), may hold values from -0.1875 to 0.1875
- w_value: bfloat16 [1024, 4096], P(None, 'enc'), may hold values from -0.75 to 0.75
- enc_gain: float32 [1024], replicated, may hold values from 0.5 to 1.5
- enc_qkv: bfloat16 [1024, 3072], replicated, may hold values from -0.1875 to 0.1875
- enc_out: bfloat16 [1024, 1024], replicated, may hold values from -0.1875 to 0.1875
Outputs:
- grad_encoded: float32 [256, 128, 1024], P(('enc', 'gen'))
- grad_w_out: float32 [4096, 4096], P('enc', 'gen')
- grad_w_key: float32 [1024, 4096], P('gen', 'enc')
- grad_w_value: float32 [1024, 4096], P('gen', 'enc')
Inputs may be any that keep to these rules, and one draw needn't show every extreme that they name: `nbr_index`: every entry 0 to 255 is named exactly once. Entry p is held by index (p // 2) % 16 of gen; block c belongs to index c * 64 // 512 of gen. The blocks of one index of gen name at most 2 entries held by one index of gen, and some pair of indices reaches 2 in every draw.
All inputs are finite; a program needn't handle non-finite values.
Results may differ from a plain program's by a relative error of at most 0.038.
Values may be sent and summed in bfloat16 or wider, within the bound.
A program may use at most 128 MiB of HBM per device.

v0:
```python
import jax
import jax.numpy as jnp
from jax import lax
from jax.sharding import PartitionSpec as P

H = 32
EH = 8
CH = 64
K = 2
SOFTCAP = 5.0
EPSILON = 1e-06


def rms_scale(values, gain):
    wide = values.astype(jnp.float32)
    factor = lax.rsqrt(jnp.mean(wide * wide, axis=-1, keepdims=True) + EPSILON)
    return (wide * factor * gain).astype(jnp.bfloat16)


def attention_parts(queries, keys_all, values_all):
    head_width = queries.shape[-1]
    raw_scores = jnp.einsum(
        "bqhd,bkhd->bhqk", queries, keys_all, preferred_element_type=jnp.float32
    ) * head_width ** (-0.5)
    capped = SOFTCAP * jnp.tanh(raw_scores / SOFTCAP)
    expo_terms = jnp.exp(capped)
    probs_full = expo_terms / jnp.sum(expo_terms, axis=-1, keepdims=True)
    probs_low = probs_full.astype(jnp.bfloat16)
    mixed = jnp.einsum(
        "bhqk,bkhd->bqhd", probs_low, values_all, preferred_element_type=jnp.float32
    ).astype(jnp.bfloat16)
    return (raw_scores, probs_full, probs_low, mixed)


def attention_grads(queries, values_all, raw_scores, probs_full, probs_low, d_mixed):
    head_width = queries.shape[-1]
    d_probs = jnp.einsum("bqhd,bkhd->bhqk", d_mixed, values_all, preferred_element_type=jnp.float32)
    d_capped = probs_full * (d_probs - jnp.sum(probs_full * d_probs, axis=-1, keepdims=True))
    slope = jnp.tanh(raw_scores / SOFTCAP)
    d_raw = (d_capped * (1.0 - slope * slope) * head_width ** (-0.5)).astype(jnp.bfloat16)
    d_keys = jnp.einsum(
        "bhqk,bqhd->bkhd", d_raw, queries, preferred_element_type=jnp.float32
    ).astype(jnp.bfloat16)
    d_values = jnp.einsum(
        "bhqk,bqhd->bkhd", probs_low, d_mixed, preferred_element_type=jnp.float32
    ).astype(jnp.bfloat16)
    return (d_keys, d_values)


def encode(nbr_embed, enc_gain, enc_qkv, enc_out):
    entries, length, enc_width = nbr_embed.shape
    normed = rms_scale(nbr_embed, enc_gain).reshape(entries * length, enc_width)
    projected = jnp.dot(normed, enc_qkv, preferred_element_type=jnp.float32).astype(jnp.bfloat16)
    projected = projected.reshape(entries, length, 3, EH, enc_width // EH)
    outputs = attention_parts(projected[:, :, 0], projected[:, :, 1], projected[:, :, 2])
    attended = outputs[3].reshape(entries * length, enc_width)
    update = jnp.dot(attended, enc_out, preferred_element_type=jnp.float32).reshape(
        entries, length, enc_width
    )
    return (nbr_embed.astype(jnp.float32) + update).astype(jnp.bfloat16)


def routing(nbr_index, row_index, gen_count, per_device, row_size, capacity):
    slot_entries = nbr_index.reshape(-1)
    entry_count = slot_entries.shape[0]
    slot_ids = jnp.arange(entry_count, dtype=jnp.int32)
    target = slot_ids // row_size
    source = slot_entries // per_device % gen_count
    column = slot_entries // (per_device * gen_count) * per_device + slot_entries % per_device
    pair_ids = target * gen_count + source
    pair_onehot = (
        pair_ids[:, None] == jnp.arange(gen_count * gen_count, dtype=jnp.int32)[None, :]
    ).astype(jnp.int32)
    earlier = jnp.cumsum(pair_onehot, axis=0) - pair_onehot
    rank_in = jnp.sum(earlier * pair_onehot, axis=1)
    send_slot = target * capacity + rank_in
    buffer_ids = jnp.arange(gen_count * capacity, dtype=jnp.int32)
    is_mine = (source == row_index).astype(jnp.int32)
    send_match = (send_slot[:, None] == buffer_ids[None, :]).astype(jnp.int32) * is_mine[:, None]
    send_column = jnp.sum(send_match * column[:, None], axis=0)
    column_ids = jnp.arange(row_size, dtype=jnp.int32)
    column_match = (column[:, None] == column_ids[None, :]).astype(jnp.int32) * is_mine[:, None]
    column_position = jnp.sum(column_match * send_slot[:, None], axis=0)
    own_source = lax.dynamic_slice_in_dim(source, row_index * row_size, row_size)
    own_rank = lax.dynamic_slice_in_dim(rank_in, row_index * row_size, row_size)
    receive_position = own_source * capacity + own_rank
    receive_match = (receive_position[:, None] == buffer_ids[None, :]).astype(jnp.int32)
    position_slot = jnp.sum(receive_match * column_ids[:, None], axis=0)
    return (send_column, column_position, receive_position, position_slot)


def local(
    hidden_states,
    grad_out,
    nbr_embed,
    nbr_index,
    gain,
    w_query,
    w_out,
    w_key,
    w_value,
    enc_gain,
    enc_qkv,
    enc_out,
):
    enc_count = lax.axis_size("enc")
    gen_count = lax.axis_size("gen")
    row_index = lax.axis_index("gen")
    per_device, length, enc_width = nbr_embed.shape
    row_size = per_device * enc_count
    capacity = max(2, 2 * row_size // gen_count)
    token_count, model_width = hidden_states.shape
    head_feats = w_query.shape[1]
    head_width = model_width // H
    head_count = head_feats // head_width
    block_count = token_count // CH
    send_column, column_position, receive_position, position_slot = routing(
        nbr_index, row_index, gen_count, per_device, row_size, capacity
    )
    encoded = encode(nbr_embed, enc_gain, enc_qkv, enc_out)
    row_encoded = lax.all_gather(encoded, "enc", axis=0, tiled=True)
    outgoing = jnp.take(row_encoded, send_column, axis=0)
    incoming = lax.all_to_all(outgoing, "gen", split_axis=0, concat_axis=0, tiled=True)
    slot_encoded = jnp.take(incoming, receive_position, axis=0)
    slot_rows = slot_encoded.reshape(row_size * length, enc_width)
    normed = rms_scale(hidden_states, gain)
    queries = jnp.dot(normed, w_query, preferred_element_type=jnp.float32).astype(jnp.bfloat16)
    queries = queries.reshape(block_count, CH, head_count, head_width)
    keys_all = jnp.dot(slot_rows, w_key, preferred_element_type=jnp.float32).astype(jnp.bfloat16)
    values_all = jnp.dot(slot_rows, w_value, preferred_element_type=jnp.float32).astype(
        jnp.bfloat16
    )
    keys_all = keys_all.reshape(block_count, K * length, head_count, head_width)
    values_all = values_all.reshape(block_count, K * length, head_count, head_width)
    raw_scores, probs_full, probs_low, mixed = attention_parts(queries, keys_all, values_all)
    mixed_rows = mixed.reshape(token_count, head_feats)
    d_mixed = jnp.dot(grad_out, w_out.T, preferred_element_type=jnp.float32).astype(jnp.bfloat16)
    out_term = jnp.dot(mixed_rows.T, grad_out, preferred_element_type=jnp.float32)
    d_keys, d_values = attention_grads(
        queries,
        values_all,
        raw_scores,
        probs_full,
        probs_low,
        d_mixed.reshape(block_count, CH, head_count, head_width),
    )
    d_keys_rows = d_keys.reshape(row_size * length, head_feats)
    d_values_rows = d_values.reshape(row_size * length, head_feats)
    key_term = jnp.dot(slot_rows.T, d_keys_rows, preferred_element_type=jnp.float32)
    value_term = jnp.dot(slot_rows.T, d_values_rows, preferred_element_type=jnp.float32)
    enc_term = jnp.dot(d_keys_rows, w_key.T, preferred_element_type=jnp.float32) + jnp.dot(
        d_values_rows, w_value.T, preferred_element_type=jnp.float32
    )
    enc_term_low = enc_term.astype(jnp.bfloat16).reshape(row_size, length, enc_width)
    returning = jnp.take(enc_term_low, position_slot, axis=0)
    returned = lax.all_to_all(returning, "gen", split_axis=0, concat_axis=0, tiled=True)
    row_grads = jnp.take(returned, column_position, axis=0).astype(jnp.float32)
    grad_encoded = lax.psum_scatter(
        row_grads.astype(jnp.bfloat16), "enc", scatter_dimension=0, tiled=True
    ).astype(jnp.float32)
    grad_w_out, grad_w_key, grad_w_value = (
        lax.psum_scatter(
            out_term.astype(jnp.bfloat16), "gen", scatter_dimension=1, tiled=True
        ).astype(jnp.float32),
        lax.psum_scatter(
            key_term.astype(jnp.bfloat16), "gen", scatter_dimension=0, tiled=True
        ).astype(jnp.float32),
        lax.psum_scatter(
            value_term.astype(jnp.bfloat16), "gen", scatter_dimension=0, tiled=True
        ).astype(jnp.float32),
    )
    return (grad_encoded, grad_w_out, grad_w_key, grad_w_value)


def solution(mesh):
    return jax.shard_map(
        local,
        mesh=mesh,
        in_specs=(
            P("gen", None),
            P("gen", None),
            P(("enc", "gen"), None, None),
            P(),
            P(),
            P(None, "enc"),
            P("enc", None),
            P(None, "enc"),
            P(None, "enc"),
            P(),
            P(),
            P(),
        ),
        out_specs=(
            P(("enc", "gen"), None, None),
            P("enc", "gen"),
            P("gen", "enc"),
            P("gen", "enc"),
        ),
        check_vma=False,
    )
```

profile of v0, /device:TPU:0, one launch (start us, length us, event | category | flops | bytes accessed | tf_op | source)
XLA Modules:
  0.0 657.2 jit_solution(7774443420112423372)
XLA Ops:
  7.2 1.4 fusion.41
  8.6 1.2 fusion.43
  9.8 4.6 fusion.23
  16.9 2.5 fusion.26
  19.5 2.1 convolution_convert_fusion.7
  21.6 1.5 fusion.29
  24.4 33.7 %all-gather.2.cloned.1.call-done = bf16[16,128,1024]{2,1,0:T(8,128)(2,1)} async-done(((bf16[2,128,1024]{2,1,0:T(8,128)(2,1)}), bf16[16,128,1024]{2,1,0:T(8,128)(2,1)}) %all-gather.2.cloned.1.call-update) | async-done | bytes 4194320 | tf_op jit(solution)/shard_map/all_gather | solution.py:121
  58.1 7.1 %gather_fusion = bf16[32,128,1024]{2,1,0:T(8,128)(2,1)} fusion(bf16[16,128,1024]{2,1,0:T(8,128)(2,1)} %all-gather.2.cloned.1.call-done, s32[1024]{0:T(1024)S(1)} %pad_clamp_fusion.3), kind=kCustom, calls=%fused_computation.clone | custom fusion | bytes 16777344 | tf_op jit(solution)/shard_map/jit(_take)/gather | solution.py:122
  65.1 7.5 %broadcast_select_fusion.1 = bf16[32,128,1024]{2,1,0:T(8,128)(2,1)} fusion(bf16[32,128,1024]{2,1,0:T(8,128)(2,1)} %gather_fusion, pred[32]{0:T(512)(128)(4,1)S(1)} %compare_and_fusion.3), kind=kLoop, calls=%fused_computation.12 | loop fusion | flops 4194304 | bytes 16777248 | tf_op jit(solution)/shard_map/jit(_take)/select_n | solution.py:122
  72.6 7.0 %all-to-all-start = ((bf16[32,128,1024]{2,1,0:T(8,128)(2,1)}), bf16[32,128,1024]{2,1,0:T(8,128)(2,1)}, u32[]{:S(2)}, u32[]{:S(2)}) async-start(bf16[32,128,1024]{2,1,0:T(8,128)(2,1)} %broadcast_select_fusion.1), calls=%async_computation | async-start | bytes 16777216 | tf_op jit(solution)/shard_map/all_to_all | solution.py:123
  80.1 3.2 fusion.1
  83.6 4.6 fusion.35
  88.3 5.8 convolution_convert_fusion.6
  94.3 133.0 %all-to-all-done = bf16[32,128,1024]{2,1,0:T(8,128)(2,1)} async-done(((bf16[32,128,1024]{2,1,0:T(8,128)(2,1)}), bf16[32,128,1024]{2,1,0:T(8,128)(2,1)}, u32[]{:S(2)}, u32[]{:S(2)}) %all-to-all-start) | async-done | bytes 8388640 | tf_op jit(solution)/shard_map/all_to_all | solution.py:123
  227.4 6.2 gather_fusion.1
  233.5 2.7 broadcast_select_fusion.3
  236.3 1.9 copy-done.5
  238.2 3.7 convolution_convert_fusion.2
  241.9 2.7 reshape.226
  244.6 6.2 convolution_convert_fusion.3
  250.8 4.0 reshape.224
  254.8 2.2 fusion.19
  257.0 2.2 fusion.22
  259.2 16.0 %convert_bitcast_fusion.1 = bf16[8,256,4,128]{1,3,2,0:T(8,128)(2,1)} fusion(f32[8,4,64,256]{3,2,1,0:T(8,128)} %fusion.19, f32[8,4,64,256]{3,2,1,0:T(8,128)} %get-tuple-element.15, bf16[8,64,4,128]{3,2,1,0:T(4,128)(2,1)S(1)} %reshape.217, f32[8,4,64]{2,1,0:T(4,128)S(1)} %get-tuple-element.14), kind=kOutput, calls=%fused_computation.27 | convolution fusion | flops 142608640 | bytes 6823936 | tf_op jit(solution)/shard_map/bhqk,bqhd->bkhd/dot_general | solution.py:41
  275.2 2.8 copy.80
  278.7 1.3 copy-done.8
  281.0 3.4 convolution_convert_fusion.5
  284.7 2.6 convert_bitcast_fusion
  287.3 1.2 copy.82
  289.2 1.4 copy-done.10
  291.5 3.5 convolution_convert_fusion.4
  295.0 2.6 fusion.38
  298.1 5.7 fusion.81
  303.8 4.3 convolution_convert_fusion
  308.1 8.5 %add_convert_fusion = bf16[2048,1024]{1,0:T(8,128)(2,1)} fusion(f32[2048,1024]{1,0:T(8,128)} %fusion.81, bf16[2048,512]{0,1:T(8,128)(2,1)} %bitcast.96, bf16[1024,512]{1,0:T(8,128)(2,1)S(1)} %copy-done.15), kind=kOutput, calls=%fused_computation.10 | convolution fusion | flops 2151677952 | bytes 15728640 | tf_op jit(solution)/shard_map/dot_general | solution.py:151
  316.6 7.2 %gather_fusion.2 = bf16[32,128,1024]{2,1,0:T(8,128)(2,1)} fusion(bf16[16,128,1024]{2,1,0:T(8,128)(2,1)} %bitcast.84, s32[1024]{0:T(1024)S(1)} %pad_clamp_fusion.1), kind=kCustom, calls=%fused_computation.2.clone | custom fusion | bytes 16777344 | tf_op jit(solution)/shard_map/jit(_take)/gather | solution.py:155
  323.8 7.5 %broadcast_select_fusion = bf16[32,128,1024]{2,1,0:T(8,128)(2,1)} fusion(bf16[32,128,1024]{2,1,0:T(8,128)(2,1)} %gather_fusion.2, pred[32]{0:T(512)(128)(4,1)S(1)} %compare_and_fusion.1), kind=kLoop, calls=%fused_computation.11 | loop fusion | flops 4194304 | bytes 16777248 | tf_op jit(solution)/shard_map/jit(_take)/select_n | solution.py:155
  331.3 11.5 %all-to-all-start.1 = ((bf16[32,128,1024]{2,1,0:T(8,128)(2,1)}), bf16[32,128,1024]{2,1,0:T(8,128)(2,1)}, u32[]{:S(2)}, u32[]{:S(2)}) async-start(bf16[32,128,1024]{2,1,0:T(8,128)(2,1)} %broadcast_select_fusion), calls=%async_computation.1 | async-start | bytes 16777216 | tf_op jit(solution)/shard_map/all_to_all | solution.py:156
  343.0 130.1 %all-to-all-done.1 = bf16[32,128,1024]{2,1,0:T(8,128)(2,1)} async-done(((bf16[32,128,1024]{2,1,0:T(8,128)(2,1)}), bf16[32,128,1024]{2,1,0:T(8,128)(2,1)}, u32[]{:S(2)}, u32[]{:S(2)}) %all-to-all-start.1) | async-done | bytes 8388640 | tf_op jit(solution)/shard_map/all_to_all | solution.py:156
  473.1 6.2 gather_fusion.3
  479.3 4.7 broadcast_select_fusion.2
  484.0 1.6 convert_element_type.136
  485.7 41.9 %reduce-scatter.11.cloned.1.call-done = bf16[64,512]{1,0:T(8,128)(2,1)} async-done(((bf16[1024,512]{1,0:T(8,128)(2,1)}), bf16[64,512]{1,0:T(8,128)(2,1)}) %reduce-scatter.11.cloned.1.call-update) | async-done | bytes 65552 | tf_op jit(solution)/shard_map/reduce_scatter | solution.py:168
  527.6 1.5 convert_element_type.138
  529.1 79.5 %reduce-scatter.7.cloned.1.call-done = bf16[512,256]{1,0:T(8,128)(2,1)} async-done(((bf16[512,4096]{1,0:T(8,128)(2,1)}), bf16[512,256]{1,0:T(8,128)(2,1)}) %reduce-scatter.7.cloned.1.call-update) | async-done | bytes 262160 | tf_op jit(solution)/shard_map/reduce_scatter | solution.py:162
  608.6 1.8 convert_element_type.134
  610.4 38.0 %reduce-scatter.5.cloned.1.call-done = bf16[2,128,1024]{2,1,0:T(8,128)(2,1)} async-done(((bf16[16,128,1024]{2,1,0:T(8,128)(2,1)}), bf16[2,128,1024]{2,1,0:T(8,128)(2,1)}) %reduce-scatter.5.cloned.1.call-update) | async-done | bytes 524304 | tf_op jit(solution)/shard_map/reduce_scatter | solution.py:158
  648.3 2.1 convert_element_type.130
  (83 shorter events, 9.0 us)
Async XLA Ops:
  7.2 14.4 %copy-start = (bf16[1024,1024]{1,0:T(8,128)(2,1)S(1)}, bf16[1024,1024]{1,0:T(8,128)(2,1)}, u32[]{:S(2)}) copy-start(bf16[1024,1024]{1,0:T(8,128)(2,1)} %param.27) | copy-start | bytes 6291460
  7.2 50.9 %all-gather.2.cloned.1.call-start = ((), (), s32[]{:S(2)}) async-start(), calls=%async_computation.6 | async-start | bytes 4718592 | tf_op jit(solution)/shard_map/all_gather | solution.py:121
  19.5 2.1 copy-start.2
  21.6 1.6 copy-start.12
  72.6 10.8 %copy-start.16 = (f32[4096]{0:T(1024)S(1)}, f32[4096]{0:T(1024)}, u32[]{:S(2)}) copy-start(f32[4096]{0:T(1024)} %param.20) | copy-start | bytes 49156
  72.6 154.7 %all-to-all-start = ((bf16[32,128,1024]{2,1,0:T(8,128)(2,1)}), bf16[32,128,1024]{2,1,0:T(8,128)(2,1)}, u32[]{:S(2)}, u32[]{:S(2)}) async-start(bf16[32,128,1024]{2,1,0:T(8,128)(2,1)} %broadcast_select_fusion.1), calls=%async_computation | async-start | bytes 16777216 | tf_op jit(solution)/shard_map/all_to_all | solution.py:123
  79.6 404.4 %reduce-scatter.9.cloned.1.call-start = ((), (), s32[]{:S(2)}) async-start(), calls=%async_computation.9 | async-start | bytes 1114112 | tf_op jit(solution)/shard_map/reduce_scatter | solution.py:165
  80.1 3.5 copy-start.3
  233.5 4.7 copy-start.14
  236.3 1.9 copy-start.5
  254.8 2.2 copy-start.11
  278.0 2.9 copy-start.6
  278.7 1.3 copy-start.8
  284.3 243.3 %reduce-scatter.11.cloned.1.call-start = ((), (), s32[]{:S(2)}) async-start(), calls=%async_computation.10 | async-start | bytes 1114112 | tf_op jit(solution)/shard_map/reduce_scatter | solution.py:168
  288.5 2.9 copy-start.7
  289.2 1.4 copy-start.10
  295.0 313.6 %reduce-scatter.7.cloned.1.call-start = ((), (), s32[]{:S(2)}) async-start(), calls=%async_computation.8 | async-start | bytes 4456448 | tf_op jit(solution)/shard_map/reduce_scatter | solution.py:162
  295.0 3.1 copy-start.9
  295.0 3.1 copy-start.13
  298.1 5.7 copy-start.4
  303.8 4.3 copy-start.15
  331.3 141.8 %all-to-all-start.1 = ((bf16[32,128,1024]{2,1,0:T(8,128)(2,1)}), bf16[32,128,1024]{2,1,0:T(8,128)(2,1)}, u32[]{:S(2)}, u32[]{:S(2)}) async-start(bf16[32,128,1024]{2,1,0:T(8,128)(2,1)} %broadcast_select_fusion), calls=%async_computation.1 | async-start | bytes 16777216 | tf_op jit(solution)/shard_map/all_to_all | solution.py:156
  342.8 305.5 %reduce-scatter.5.cloned.1.call-start = ((), (), s32[]{:S(2)}) async-start(), calls=%async_computation.7 | async-start | bytes 4718592 | tf_op jit(solution)/shard_map/reduce_scatter | solution.py:158
  484.0 166.5 %copy-start.1 = (bf16[1024,1024]{1,0:T(8,128)(2,1)S(1)}, bf16[1024,1024]{1,0:T(8,128)(2,1)}, u32[]{:S(2)}) copy-start(bf16[1024,1024]{1,0:T(8,128)(2,1)} %param.27) | copy-start | bytes 6291460
Sparse Core Ops, SparseCore 0:
  23.3 34.7 all-gather.1
  284.5 121.2 reduce-scatter.8
  409.0 118.6 reduce-scatter.10
  530.8 77.7 reduce-scatter.6
  610.8 37.4 reduce-scatter.4
where the time goes:
time: 663 us; the launch traced here: 657 us
  waiting for transfers between devices  456 us (69%)
  matrix products  82 us (12%)
  local copies, waits for them, and re-layouts  48.9 us (7%)
  other arithmetic  36.3 us (5%)
  starting transfers between devices  19.4 us (3%)
  between operations  14.4 us (2%)
    all_to_all x1, waiting for transfers between devices, local(): lax.all_to_all(outgoing, 'gen', split_axis=0, concat_axis=0, tiled=True)  133 us
    all_to_all x1, waiting for transfers between devices, local(): lax.all_to_all(returning, 'gen', split_axis=0, concat_axis=0, tiled=True)  130 us
    reduce_scatter x1, waiting for transfers between devices, local(): lax.psum_scatter(out_term.astype(jnp.bfloat16), 'gen', scatter_dimension=...  79.5 us
    reduce_scatter x1, waiting for transfers between devices, local(): lax.psum_scatter(value_term.astype(jnp.bfloat16), 'gen', scatter_dimensio...  41.9 us
    reduce_scatter x1, waiting for transfers between devices, local(): lax.psum_scatter(row_grads.astype(jnp.bfloat16), 'enc', scatter_dimension...  38 us
    all_gather x1, waiting for transfers between devices, local(): row_encoded = lax.all_gather(encoded, 'enc', axis=0, tiled=True)  33.7 us
    dot_general x1, matrix products, attention_grads(): jnp.einsum('bhqk,bqhd->bkhd', d_raw, queries, preferred_element_type=jnp....  16 us
  transfers between devices with their start and end apart: 7, of which 6 were waited for; matrix products, arithmetic and copies ran while one was open for 11% of the time, Pallas kernels for 0%

commit v1 on v0

--- a/solution.py
+++ b/solution.py
@@ -103,6 +103,16 @@
     enc_qkv,
     enc_out,
 ):
+
+    def press_point(original, axis_id):
+        trail = []
+        for _ in range(lax.axis_size(axis_id)):
+            trail.append(original)
+        piece_now = jnp.stack(trail, axis=0)
+        u1 = lax.all_to_all(piece_now, axis_name=axis_id, split_axis=0, concat_axis=0)
+        o_now = jnp.concatenate(u1, axis=0)
+        return o_now
+
     enc_count = lax.axis_size("enc")
     gen_count = lax.axis_size("gen")
     row_index = lax.axis_index("gen")
@@ -118,7 +128,7 @@
         nbr_index, row_index, gen_count, per_device, row_size, capacity
     )
     encoded = encode(nbr_embed, enc_gain, enc_qkv, enc_out)
-    row_encoded = lax.all_gather(encoded, "enc", axis=0, tiled=True)
+    row_encoded = press_point(encoded, "enc")
     outgoing = jnp.take(row_encoded, send_column, axis=0)
     incoming = lax.all_to_all(outgoing, "gen", split_axis=0, concat_axis=0, tiled=True)
     slot_encoded = jnp.take(incoming, receive_position, axis=0)

time: 663 us -> 695 us (1.048)
  waiting for transfers between devices: 456 us -> 482 us
    all_to_all x0 -> x1, waiting for transfers between devices: none -> 48.5 us  [press_point(): lax.all_to_all(piece_now, axis_name=axis_id, split_axis=0, concat_axis=0)]
    all_gather x1 -> x0, waiting for transfers between devices: 33.7 us -> none  [local(): row_encoded = lax.all_gather(encoded, 'enc', axis=0, tiled=True)]
    reduce_scatter x1, waiting for transfers between devices: 41.9 us -> 69 us  [local(): lax.psum_scatter(value_term.astype(jnp.bfloat16), 'gen', scatter_dimensio...]
    all_to_all x1, waiting for transfers between devices: 130 us -> 117 us  [local(): lax.all_to_all(returning, 'gen', split_axis=0, concat_axis=0, tiled=True)]
where the time goes in v1:
time: 695 us; the launch traced here: 688 us
  waiting for transfers between devices  482 us (69%)
  matrix products  81.2 us (12%)
  local copies, waits for them, and re-layouts  51.4 us (7%)
  other arithmetic  36.2 us (5%)
  starting transfers between devices  23.4 us (3%)
  between operations  14.4 us (2%)
    all_to_all x1, waiting for transfers between devices, local(): lax.all_to_all(outgoing, 'gen', split_axis=0, concat_axis=0, tiled=True)  129 us
    all_to_all x1, waiting for transfers between devices, local(): lax.all_to_all(returning, 'gen', split_axis=0, concat_axis=0, tiled=True)  117 us
    reduce_scatter x1, waiting for transfers between devices, local(): lax.psum_scatter(out_term.astype(jnp.bfloat16), 'gen', scatter_dimension=...  79.7 us
    reduce_scatter x1, waiting for transfers between devices, local(): lax.psum_scatter(value_term.astype(jnp.bfloat16), 'gen', scatter_dimensio...  69 us
    all_to_all x1, waiting for transfers between devices, press_point(): lax.all_to_all(piece_now, axis_name=axis_id, split_axis=0, concat_axis=0)  48.5 us
    reduce_scatter x1, waiting for transfers between devices, local(): lax.psum_scatter(row_grads.astype(jnp.bfloat16), 'enc', scatter_dimension...  38 us
    dot_general x1, matrix products, attention_grads(): jnp.einsum('bhqk,bqhd->bkhd', d_raw, queries, preferred_element_type=jnp....  16 us
  transfers between devices with their start and end apart: 7, of which 6 were waited for; matrix products, arithmetic and copies ran while one was open for 11% of the time, Pallas kernels for 0%

profile of v1, /device:TPU:0, one launch (start us, length us, event | category | flops | bytes accessed | tf_op | source)
XLA Modules:
  0.0 688.4 jit_solution(6158156021148098062)
XLA Ops:
  7.2 1.4 fusion.41
  8.6 1.2 fusion.43
  9.8 4.6 fusion.23
  16.9 2.5 fusion.26
  19.5 2.1 convolution_convert_fusion.7
  22.3 2.5 stack.2
  24.8 5.5 all-to-all-start
  31.6 48.5 %all-to-all-done = bf16[8,2,128,1024]{3,2,1,0:T(8,128)(2,1)} async-done(((bf16[8,2,128,1024]{3,2,1,0:T(8,128)(2,1)}), bf16[8,2,128,1024]{3,2,1,0:T(8,128)(2,1)}, u32[]{:S(2)}, u32[]{:S(2)}) %all-to-all-start) | async-done | bytes 4194336 | tf_op jit(solution)/shard_map/all_to_all | solution.py:112
  80.1 7.1 %gather_fusion = bf16[32,128,1024]{2,1,0:T(8,128)(2,1)} fusion(bf16[16,128,1024]{2,1,0:T(8,128)(2,1)} %bitcast.10, s32[1024]{0:T(1024)S(1)} %pad_clamp_fusion.3), kind=kCustom, calls=%fused_computation.clone | custom fusion | bytes 16777344 | tf_op jit(solution)/shard_map/jit(_take)/gather | solution.py:132
  87.2 7.5 %broadcast_select_fusion.1 = bf16[32,128,1024]{2,1,0:T(8,128)(2,1)} fusion(bf16[32,128,1024]{2,1,0:T(8,128)(2,1)} %gather_fusion, pred[32]{0:T(512)(128)(4,1)S(1)} %compare_and_fusion.3), kind=kLoop, calls=%fused_computation.12 | loop fusion | flops 4194304 | bytes 16777248 | tf_op jit(solution)/shard_map/jit(_take)/select_n | solution.py:132
  94.6 7.2 %all-to-all-start.1 = ((bf16[32,128,1024]{2,1,0:T(8,128)(2,1)}), bf16[32,128,1024]{2,1,0:T(8,128)(2,1)}, u32[]{:S(2)}, u32[]{:S(2)}) async-start(bf16[32,128,1024]{2,1,0:T(8,128)(2,1)} %broadcast_select_fusion.1), calls=%async_computation.1 | async-start | bytes 16777216 | tf_op jit(solution)/shard_map/all_to_all | solution.py:133
  102.4 3.2 fusion.1
  105.8 4.6 fusion.35
  110.5 5.8 convolution_convert_fusion.6
  116.6 129.3 %all-to-all-done.1 = bf16[32,128,1024]{2,1,0:T(8,128)(2,1)} async-done(((bf16[32,128,1024]{2,1,0:T(8,128)(2,1)}), bf16[32,128,1024]{2,1,0:T(8,128)(2,1)}, u32[]{:S(2)}, u32[]{:S(2)}) %all-to-all-start.1) | async-done | bytes 8388640 | tf_op jit(solution)/shard_map/all_to_all | solution.py:133
  245.9 6.2 gather_fusion.1
  252.0 2.7 broadcast_select_fusion.3
  254.8 1.9 copy-done.5
  256.7 3.7 convolution_convert_fusion.2
  260.4 2.7 reshape.232
  263.2 6.2 convolution_convert_fusion.3
  269.3 4.0 reshape.230
  273.3 2.2 fusion.19
  275.5 2.2 fusion.22
  277.7 16.0 %convert_bitcast_fusion.1 = bf16[8,256,4,128]{1,3,2,0:T(8,128)(2,1)} fusion(f32[8,4,64,256]{3,2,1,0:T(8,128)} %fusion.19, f32[8,4,64,256]{3,2,1,0:T(8,128)} %get-tuple-element.15, bf16[8,64,4,128]{3,2,1,0:T(4,128)(2,1)S(1)} %reshape.222, f32[8,4,64]{2,1,0:T(4,128)S(1)} %get-tuple-element.14), kind=kOutput, calls=%fused_computation.27 | convolution fusion | flops 142608640 | bytes 6823936 | tf_op jit(solution)/shard_map/bhqk,bqhd->bkhd/dot_general | solution.py:41
  293.8 2.8 copy.61
  297.2 1.3 copy-done.8
  299.5 3.4 convolution_convert_fusion.5
  303.2 2.6 convert_bitcast_fusion
  307.8 1.4 copy-done.10
  310.0 3.5 convolution_convert_fusion.4
  313.6 2.6 fusion.38
  316.7 5.7 fusion.81
  322.3 4.3 convolution_convert_fusion
  326.6 8.5 %add_convert_fusion = bf16[2048,1024]{1,0:T(8,128)(2,1)} fusion(f32[2048,1024]{1,0:T(8,128)} %fusion.81, bf16[2048,512]{0,1:T(8,128)(2,1)} %bitcast.97, bf16[1024,512]{1,0:T(8,128)(2,1)S(1)} %copy-done.15), kind=kOutput, calls=%fused_computation.10 | convolution fusion | flops 2151677952 | bytes 15728640 | tf_op jit(solution)/shard_map/dot_general | solution.py:161
  335.1 7.1 %gather_fusion.2 = bf16[32,128,1024]{2,1,0:T(8,128)(2,1)} fusion(bf16[16,128,1024]{2,1,0:T(8,128)(2,1)} %bitcast.85, s32[1024]{0:T(1024)S(1)} %pad_clamp_fusion.1), kind=kCustom, calls=%fused_computation.2.clone | custom fusion | bytes 16777344 | tf_op jit(solution)/shard_map/jit(_take)/gather | solution.py:165
  342.2 7.5 %broadcast_select_fusion = bf16[32,128,1024]{2,1,0:T(8,128)(2,1)} fusion(bf16[32,128,1024]{2,1,0:T(8,128)(2,1)} %gather_fusion.2, pred[32]{0:T(512)(128)(4,1)S(1)} %compare_and_fusion.1), kind=kLoop, calls=%fused_computation.11 | loop fusion | flops 4194304 | bytes 16777248 | tf_op jit(solution)/shard_map/jit(_take)/select_n | solution.py:165
  349.7 9.8 %all-to-all-start.2 = ((bf16[32,128,1024]{2,1,0:T(8,128)(2,1)}), bf16[32,128,1024]{2,1,0:T(8,128)(2,1)}, u32[]{:S(2)}, u32[]{:S(2)}) async-start(bf16[32,128,1024]{2,1,0:T(8,128)(2,1)} %broadcast_select_fusion), calls=%async_computation.2 | async-start | bytes 16777216 | tf_op jit(solution)/shard_map/all_to_all | solution.py:166
  359.8 117.2 %all-to-all-done.2 = bf16[32,128,1024]{2,1,0:T(8,128)(2,1)} async-done(((bf16[32,128,1024]{2,1,0:T(8,128)(2,1)}), bf16[32,128,1024]{2,1,0:T(8,128)(2,1)}, u32[]{:S(2)}, u32[]{:S(2)}) %all-to-all-start.2) | async-done | bytes 8388640 | tf_op jit(solution)/shard_map/all_to_all | solution.py:166
  477.0 6.2 gather_fusion.3
  483.2 4.7 broadcast_select_fusion.2
  487.9 1.6 convert_element_type.136
  489.5 69.0 %reduce-scatter.11.cloned.1.call-done = bf16[64,512]{1,0:T(8,128)(2,1)} async-done(((bf16[1024,512]{1,0:T(8,128)(2,1)}), bf16[64,512]{1,0:T(8,128)(2,1)}) %reduce-scatter.11.cloned.1.call-update) | async-done | bytes 65552 | tf_op jit(solution)/shard_map/reduce_scatter | solution.py:178
  558.5 1.5 convert_element_type.138
  560.0 79.7 %reduce-scatter.7.cloned.1.call-done = bf16[512,256]{1,0:T(8,128)(2,1)} async-done(((bf16[512,4096]{1,0:T(8,128)(2,1)}), bf16[512,256]{1,0:T(8,128)(2,1)}) %reduce-scatter.7.cloned.1.call-update) | async-done | bytes 262160 | tf_op jit(solution)/shard_map/reduce_scatter | solution.py:172
  639.7 1.8 convert_element_type.134
  641.5 38.0 %reduce-scatter.5.cloned.1.call-done = bf16[2,128,1024]{2,1,0:T(8,128)(2,1)} async-done(((bf16[16,128,1024]{2,1,0:T(8,128)(2,1)}), bf16[2,128,1024]{2,1,0:T(8,128)(2,1)}) %reduce-scatter.5.cloned.1.call-update) | async-done | bytes 524304 | tf_op jit(solution)/shard_map/reduce_scatter | solution.py:168
  679.5 2.1 convert_element_type.130
  (83 shorter events, 10.9 us)
Async XLA Ops:
  7.2 14.4 %copy-start = (bf16[1024,1024]{1,0:T(8,128)(2,1)S(1)}, bf16[1024,1024]{1,0:T(8,128)(2,1)}, u32[]{:S(2)}) copy-start(bf16[1024,1024]{1,0:T(8,128)(2,1)} %param.27) | copy-start | bytes 6291460
  19.5 2.1 copy-start.2
  24.8 5.5 copy-start.12
  24.8 55.3 %all-to-all-start = ((bf16[8,2,128,1024]{3,2,1,0:T(8,128)(2,1)}), bf16[8,2,128,1024]{3,2,1,0:T(8,128)(2,1)}, u32[]{:S(2)}, u32[]{:S(2)}) async-start(bf16[8,2,128,1024]{3,2,1,0:T(8,128)(2,1)} %stack.2), calls=%async_computation | async-start | bytes 8388608 | tf_op jit(solution)/shard_map/all_to_all | solution.py:112
  94.6 11.0 %copy-start.16 = (f32[4096]{0:T(1024)S(1)}, f32[4096]{0:T(1024)}, u32[]{:S(2)}) copy-start(f32[4096]{0:T(1024)} %param.20) | copy-start | bytes 49156
  94.6 151.2 %all-to-all-start.1 = ((bf16[32,128,1024]{2,1,0:T(8,128)(2,1)}), bf16[32,128,1024]{2,1,0:T(8,128)(2,1)}, u32[]{:S(2)}, u32[]{:S(2)}) async-start(bf16[32,128,1024]{2,1,0:T(8,128)(2,1)} %broadcast_select_fusion.1), calls=%async_computation.1 | async-start | bytes 16777216 | tf_op jit(solution)/shard_map/all_to_all | solution.py:133
  101.9 386.0 %reduce-scatter.9.cloned.1.call-start = ((), (), s32[]{:S(2)}) async-start(), calls=%async_computation.9 | async-start | bytes 1114112 | tf_op jit(solution)/shard_map/reduce_scatter | solution.py:175
  102.4 3.5 copy-start.3
  252.0 4.7 copy-start.14
  254.8 1.9 copy-start.5
  273.3 2.2 copy-start.11
  296.5 2.9 copy-start.6
  297.2 1.3 copy-start.8
  302.9 255.7 %reduce-scatter.11.cloned.1.call-start = ((), (), s32[]{:S(2)}) async-start(), calls=%async_computation.10 | async-start | bytes 1114112 | tf_op jit(solution)/shard_map/reduce_scatter | solution.py:178
  307.1 2.9 copy-start.7
  307.8 1.4 copy-start.10
  313.5 326.3 %reduce-scatter.7.cloned.1.call-start = ((), (), s32[]{:S(2)}) async-start(), calls=%async_computation.8 | async-start | bytes 4456448 | tf_op jit(solution)/shard_map/reduce_scatter | solution.py:172
  313.5 3.1 copy-start.9
  313.6 3.1 copy-start.13
  316.6 5.7 copy-start.4
  322.3 4.3 copy-start.15
  349.7 127.3 %all-to-all-start.2 = ((bf16[32,128,1024]{2,1,0:T(8,128)(2,1)}), bf16[32,128,1024]{2,1,0:T(8,128)(2,1)}, u32[]{:S(2)}, u32[]{:S(2)}) async-start(bf16[32,128,1024]{2,1,0:T(8,128)(2,1)} %broadcast_select_fusion), calls=%async_computation.2 | async-start | bytes 16777216 | tf_op jit(solution)/shard_map/all_to_all | solution.py:166
  359.6 319.9 %reduce-scatter.5.cloned.1.call-start = ((), (), s32[]{:S(2)}) async-start(), calls=%async_computation.7 | async-start | bytes 4718592 | tf_op jit(solution)/shard_map/reduce_scatter | solution.py:168
  487.9 193.8 %copy-start.1 = (bf16[1024,1024]{1,0:T(8,128)(2,1)S(1)}, bf16[1024,1024]{1,0:T(8,128)(2,1)}, u32[]{:S(2)}) copy-start(bf16[1024,1024]{1,0:T(8,128)(2,1)} %param.27) | copy-start | bytes 6291460
Sparse Core Ops, SparseCore 0:
  303.0 138.3 reduce-scatter.8
  444.6 113.9 reduce-scatter.10
  561.9 77.8 reduce-scatter.6
  642.0 37.4 reduce-scatter.4
